TPU v7x, 128 devices: a whole 4x4x4 slice. The times are simulated.
128 devices in a mesh: head: 2 (over y_hi), block: 2 (over y_lo), tok: 32 (over z, x, core).
Axes of the slice: x: 4, y: 4 (y_hi: 2, y_lo: 2; y = y_hi * 2 + y_lo), z: 4, core: 2. Of those that a mesh axis runs over, the one named last changes fastest.
Arguments:
- tokens: bfloat16 [2, 16384, 2048], P('block', 'tok'), may hold values from -6 to 6
- input_weight: bfloat16 [2048, 3, 2048], P(None, None, 'head'), may hold values from -0.125 to 0.125
- rate_weight: bfloat16 [2048, 4], P(None, 'head'), may hold values from -0.375 to 0.375
- fast_init: bfloat16 [4, 3, 512, 512], P('head'), may hold values from -0.25 to 0.25
- output_weight: bfloat16 [2048, 2048], P('head'), may hold values from -0.125 to 0.125
Outputs:
- mixed: bfloat16 [2, 16384, 2048], P('block', 'tok', 'head')
All inputs are finite; a program needn't handle non-finite values.
Results may differ from a plain program's by a relative error of at most 0.005.
Values sent between devices are 32-bit elements; how exact they have to be, the bound alone decides.
A program may use at most 128 MiB of HBM per device.

v0:
```python
import jax
import jax.numpy as jnp
from jax import lax
from jax.sharding import PartitionSpec as P

epsilon = 1e-06
step_size = 0.03
highest = lax.Precision.HIGHEST


def passed_along(block, axis, distance):
    devices = range(lax.axis_size(axis))
    route = [(i - distance, i) for i in devices if i - distance in devices]
    return lax.ppermute(block, axis, route)


def matmul(left, right):
    return jnp.dot(left, right, precision=highest, preferred_element_type=jnp.float32)


def normalize(values):
    return values / jnp.sqrt(jnp.mean(values * values, axis=-1, keepdims=True) + epsilon)


def fast_grad(weights, keys, targets):
    gate = matmul(keys, weights[0])
    upper = matmul(keys, weights[1])
    sigma = jax.nn.sigmoid(gate)
    active = gate * sigma
    hidden = active * upper
    grad_down = matmul(targets.T, hidden)
    back = matmul(targets, weights[2])
    grad_upper = matmul(keys.T, back * active)
    grad_gate = matmul(keys.T, back * upper * sigma * (1.0 + gate * (1.0 - sigma)))
    return jnp.stack([grad_gate, grad_upper, grad_down])


def fast_apply(weights, queries):
    gate = matmul(queries, weights[0])
    upper = matmul(queries, weights[1])
    hidden = gate * jax.nn.sigmoid(gate) * upper
    return normalize(matmul(hidden, weights[2].T))


def body(tokens, input_weight, rate_weight, fast_init, output_weight):
    block_count, tok_rows, model_width = tokens.shape
    head_count, _, head_dim, fast_dim = fast_init.shape
    start_weights = fast_init.astype(jnp.float32)
    flattened = tokens.reshape(block_count * tok_rows, model_width)
    projected = jnp.dot(
        flattened, input_weight.reshape(model_width, -1), preferred_element_type=jnp.float32
    )
    projected = projected.reshape(block_count, tok_rows, 3, head_count, head_dim)
    rates = jax.nn.softplus(jnp.dot(flattened, rate_weight, preferred_element_type=jnp.float32))
    rates = rates.reshape(block_count, tok_rows, head_count)
    queries = normalize(projected[:, :, 0])
    keys = normalize(projected[:, :, 1])
    targets = projected[:, :, 2] * rates[:, :, :, None]
    base_rms = jnp.sqrt(jnp.mean(start_weights * start_weights, axis=2, keepdims=True))
    head_grads = jax.vmap(fast_grad, in_axes=(0, 1, 1))
    position = lax.axis_index("block")
    groups = lax.axis_size("block")
    chosen = [start_weights]
    incoming = start_weights
    for section in range(groups):
        weights = incoming
        local = 0
        partial_value = head_grads(weights, keys[local], targets[local])
        pieces = lax.psum_scatter(partial_value, "tok", scatter_dimension=3, tiled=True)
        width = pieces.shape[3]
        squares = jnp.sum(pieces * pieces, axis=(2, 3))
        total_sq = lax.psum(squares, "tok")
        scale = jnp.sqrt(total_sq / (head_dim * fast_dim) + epsilon)[:, :, None, None]
        start = lax.axis_index("tok") * width
        own_weights = lax.dynamic_slice_in_dim(weights, start, width, 3)
        own_rms = lax.dynamic_slice_in_dim(base_rms, start, width, 3)
        moved = own_weights + step_size * pieces / scale
        fresh = moved * own_rms / jnp.sqrt(jnp.mean(moved * moved, axis=2, keepdims=True) + epsilon)
        weights = lax.all_gather(fresh, "tok", axis=3, tiled=True)
        chosen[local] = jnp.where(position == section, weights, chosen[local])
        if section + 1 < groups:
            incoming = passed_along(weights, "block", 1)
    head_apply = jax.vmap(fast_apply, in_axes=(0, 1), out_axes=1)
    joined = []
    local = 0
    applied = head_apply(chosen[local], queries[local])
    joined.append(applied.reshape(tok_rows, head_count * head_dim))
    joined = (
        jnp.stack(joined)
        .reshape(block_count * tok_rows, head_count * head_dim)
        .astype(jnp.bfloat16)
    )
    partial_out = jnp.dot(joined, output_weight, preferred_element_type=jnp.float32)
    partial_out = partial_out.reshape(block_count, tok_rows, model_width)
    return lax.psum_scatter(partial_out, "head", scatter_dimension=2, tiled=True).astype(
        jnp.bfloat16
    )


def solution(mesh):
    placed = (
        P("block", "tok", None),
        P(None, None, "head"),
        P(None, "head"),
        P("head", None, None, None),
        P("head", None),
    )
    return jax.shard_map(
        body, mesh=mesh, in_specs=placed, out_specs=P("block", "tok", "head"), check_vma=False
    )
```

profile of v0, /device:TPU:1, one launch (start us, length us, event | category | flops | bytes accessed | tf_op | source)
XLA Modules:
  0.0 829.3 jit_solution(6733005602457865795)
XLA Ops:
  6.5 17.1 %copy.79 = bf16[2048,3,1024]{0,2,1:T(8,128)(2,1)} copy(bf16[2048,3,1024]{2,0,1:T(8,128)(2,1)} %param.6) | data formatting | bytes 25165824 | tf_op args[1]
  23.6 9.5 %convolution_bitcast_fusion.1 = f32[1,512,3,2,512]{1,4,3,2,0:T(8,128)S(1)} fusion(bf16[3,2,512,2048]{3,2,1,0:T(8,128)(2,1)} %bitcast.143, bf16[1,512,2048]{2,1,0:T(8,128)(2,1)S(1)} %copy-done), kind=kOutput, calls=%fused_computation.5 | convolution fusion | flops 6442450944 | bytes 20971520 | tf_op jit(solution)/shard_map/dot_general | solution.py:50
  33.7 3.6 copy-done.4
  37.3 1.8 fusion.82
  39.2 1.8 fusion.84
  41.0 0.7 compare_select_fusion
  41.7 1.8 fusion.80
  43.6 4.0 fusion.52
  47.5 4.5 fusion.47
  52.0 4.0 fusion.67
  56.0 3.3 maximum_bitcast_fusion
  59.3 10.3 %copy.87 = f32[2,3,512,512]{2,0,1,3:T(2,128)} copy(f32[2,3,512,512]{3,2,0,1:T(8,128)} %maximum_bitcast_fusion) | data formatting | bytes 12582912 | tf_op jit(solution)/shard_map/vmap()/transpose | solution.py:68
  69.7 3.2 copy.80
  73.0 3.5 convert_element_type.12
  76.4 0.6 dynamic-slice.4
  77.7 0.7 multiply_reduce_fusion
  78.4 110.3 %all-reduce.5.cloned.1.call-done = f32[2,3,512,512]{2,0,1,3:T(2,128)} async-done(((f32[2,3,512,512]{2,0,1,3:T(2,128)}), f32[2,3,512,512]{2,0,1,3:T(2,128)}) %all-reduce.5.cloned.1.call-update) | async-done | bytes 6291472
  188.7 1.1 multiply_reduce_fusion.7
  189.9 62.7 %psum.14 = f32[2,3]{0,1:T(4,128)S(1)} all-reduce(f32[2,3]{0,1:T(4,128)S(1)} %get-tuple-element.9), channel_id=1, replica_groups=mesh['head'=2,'block'=2,'tok'=32] {'tok'}, use_global_device_ids=true, to_apply=%region_4.5 | all-reduce | flops 6 | bytes 48 | tf_op jit(solution)/shard_map/psum | solution.py:72
  252.7 1.1 multiply_reduce_fusion.6
  253.8 1.0 multiply_divide_fusion.1
  254.8 0.8 copy.90
  255.7 49.4 %all-gather.3.cloned.1.call-done = f32[2,3,512,512]{2,0,1,3:T(2,128)} async-done(((f32[2,3,512,16]{2,0,1,3:T(2,128)}), f32[2,3,512,512]{2,0,1,3:T(2,128)}) %all-gather.3.cloned.1.call-update) | async-done | bytes 6291472 | tf_op jit(solution)/shard_map/all_gather | solution.py:79
  305.1 4.0 copy.91
  309.1 3.9 collective-permute-start
  313.0 133.8 %collective-permute-done = f32[2,3,512,512]{2,3,1,0:T(8,128)S(1)} collective-permute-done((f32[2,3,512,512]{2,3,1,0:T(8,128)S(1)}, f32[2,3,512,512]{2,3,1,0:T(8,128)S(1)}, u32[]{:S(2)}, u32[]{:S(2)}) %collective-permute-start) | collective-permute-done | bytes 6291488 | tf_op jit(solution)/shard_map/ppermute | solution.py:14
  446.8 10.1 %fusion.5 = f32[2,512,512]{2,1,0:T(8,128)S(1)} fusion(f32[2,3,512,512]{2,3,1,0:T(8,128)S(1)} %collective-permute-done, f32[1,512,3,2,512]{1,4,3,2,0:T(8,128)} %copy-done.2, f32[512,2]{0,1:T(2,128)S(1)} %compare_select_fusion), kind=kOutput, calls=%fused_computation.17 | convolution fusion | flops 3221749760 | bytes 6295552 | tf_op jit(solution)/shard_map/vmap()/dot_general | solution.py:18
  456.9 8.7 %fusion.3 = f32[2,512,512]{2,1,0:T(8,128)S(1)} fusion(f32[2,3,512,512]{2,3,1,0:T(8,128)S(1)} %collective-permute-done, f32[1,512,3,2,512]{1,4,3,2,0:T(8,128)} %copy-done.2, f32[512,2]{0,1:T(2,128)S(1)} %add_sqrt_fusion.2), kind=kOutput, calls=%fused_computation.13 | convolution fusion | flops 3221749760 | bytes 6295552 | tf_op jit(solution)/shard_map/vmap()/dot_general | solution.py:18
  465.6 4.0 fusion.62
  469.6 6.8 fusion.4
  476.4 4.5 fusion.57
  480.9 4.0 fusion.72
  484.9 3.4 maximum_bitcast_fusion.1
  488.3 10.3 %copy.98 = f32[2,3,512,512]{2,0,1,3:T(2,128)} copy(f32[2,3,512,512]{3,2,0,1:T(8,128)} %maximum_bitcast_fusion.1) | data formatting | bytes 12582912 | tf_op jit(solution)/shard_map/vmap()/transpose | solution.py:68
  498.7 115.7 %all-reduce.7.cloned.1.call-done = f32[2,3,512,512]{2,0,1,3:T(2,128)} async-done(((f32[2,3,512,512]{2,0,1,3:T(2,128)}), f32[2,3,512,512]{2,0,1,3:T(2,128)}) %all-reduce.7.cloned.1.call-update) | async-done | bytes 6291472
  614.4 1.1 multiply_reduce_fusion.5
  615.6 62.7 %psum.15 = f32[2,3]{0,1:T(4,128)S(1)} all-reduce(f32[2,3]{0,1:T(4,128)S(1)} %get-tuple-element.7), channel_id=1, replica_groups=mesh['head'=2,'block'=2,'tok'=32] {'tok'}, use_global_device_ids=true, to_apply=%region_9.10 | all-reduce | flops 6 | bytes 48 | tf_op jit(solution)/shard_map/psum | solution.py:72
  678.4 1.1 multiply_reduce_fusion.4
  679.5 1.0 multiply_divide_fusion
  680.5 0.8 copy.101
  681.9 48.9 %all-gather.5.cloned.1.call-done = f32[2,3,512,512]{2,0,1,3:T(2,128)} async-done(((f32[2,3,512,16]{2,0,1,3:T(2,128)}), f32[2,3,512,512]{2,0,1,3:T(2,128)}) %all-gather.5.cloned.1.call-update) | async-done | bytes 6291472 | tf_op jit(solution)/shard_map/all_gather | solution.py:79
  730.8 6.8 copy_select_fusion
  737.7 8.3 %fusion.2 = f32[2,512,512]{2,1,0:T(8,128)S(1)} fusion(f32[2,3,512,512]{2,3,1,0:T(8,128)S(1)} %copy_select_fusion, f32[1,512,3,2,512]{1,4,3,2,0:T(8,128)} %copy-done.2, f32[512,2]{0,1:T(2,128)S(1)} %add_sqrt_fusion.3), kind=kOutput, calls=%fused_computation.11 | convolution fusion | flops 3221749760 | bytes 6295552 | tf_op jit(solution)/shard_map/vmap()/dot_general | solution.py:18
  746.0 8.5 %fusion.1 = f32[2,512,512]{2,1,0:T(8,128)S(1)} fusion(f32[2,3,512,512]{2,3,1,0:T(8,128)S(1)} %copy_select_fusion, f32[1,512,3,2,512]{1,4,3,2,0:T(8,128)} %copy-done.2, f32[512,2]{0,1:T(2,128)S(1)} %add_sqrt_fusion.3), kind=kOutput, calls=%fused_computation.9 | convolution fusion | flops 3221749760 | bytes 6295552 | tf_op jit(solution)/shard_map/vmap()/dot_general | solution.py:18
  754.5 4.0 multiply_reduce_fusion.1
  758.8 4.3 convolution_bitcast_fusion
  763.2 56.7 %reduce-scatter.2.cloned.1.call-done = f32[1,512,1024]{2,1,0:T(8,128)} async-done(((f32[1,512,2048]{2,1,0:T(8,128)}), f32[1,512,1024]{2,1,0:T(8,128)}) %reduce-scatter.2.cloned.1.call-update) | async-done | bytes 2097168 | tf_op jit(solution)/shard_map/reduce_scatter | solution.py:95
  819.9 2.7 convert_element_type.15
  (42 shorter events, 1.9 us)
Async XLA Ops:
  6.5 17.1 %copy-start = (bf16[1,512,2048]{2,1,0:T(8,128)(2,1)S(1)}, bf16[1,512,2048]{2,1,0:T(8,128)(2,1)}, u32[]{:S(2)}) copy-start(bf16[1,512,2048]{2,1,0:T(8,128)(2,1)} %param.5) | copy-start | bytes 6291460
  6.5 182.2 %all-reduce.5.cloned.1.call-start = ((), (), s32[]{:S(2)}) async-start(), calls=%async_computation.4 | async-start | bytes 12582912
  33.1 18.9 %copy-start.2 = (f32[1,512,3,2,512]{1,4,3,2,0:T(8,128)}, f32[1,512,3,2,512]{1,4,3,2,0:T(8,128)S(1)}, u32[]{:S(2)}) copy-start(f32[1,512,3,2,512]{1,4,3,2,0:T(8,128)S(1)} %convolution_bitcast_fusion.1) | copy-start | bytes 18874372
  33.2 4.2 copy-start.4
  39.2 1.9 copy-start.6
  69.7 235.5 %all-gather.3.cloned.1.call-start = ((), (), s32[]{:S(2)}) async-start(), calls=%async_computation.1 | async-start | bytes 6488064 | tf_op jit(solution)/shard_map/all_gather | solution.py:79
  72.9 3.5 copy-start.7
  255.7 358.7 %all-reduce.7.cloned.1.call-start = ((), (), s32[]{:S(2)}) async-start(), calls=%async_computation.5 | async-start | bytes 12582912
  309.1 137.7 %collective-permute-start = (f32[2,3,512,512]{2,3,1,0:T(8,128)S(1)}, f32[2,3,512,512]{2,3,1,0:T(8,128)S(1)}, u32[]{:S(2)}, u32[]{:S(2)}) collective-permute-start(f32[2,3,512,512]{2,3,1,0:T(8,128)S(1)} %copy.91), channel_id=1, source_target_pairs={{0,32},{1,33},{2,34},{3,35},{4,36},{5,37},{6,38},{7,39},{8,40},{9,... | collective-permute-start | bytes 18874376 | tf_op jit(solution)/shard_map/ppermute | solution.py:14
  446.8 22.8 %copy-start.5 = (f32[2,3,512,512]{2,3,1,0:T(8,128)}, f32[2,3,512,512]{2,3,1,0:T(8,128)S(1)}, u32[]{:S(2)}) copy-start(f32[2,3,512,512]{2,3,1,0:T(8,128)S(1)} %collective-permute-done) | copy-start | bytes 18874372
  446.8 18.8 %slice-start = ((s8[6291456]{0:T(1024)(128)(4,1)}), s8[4194304]{0:T(1024)(128)(4,1)S(1)}, s32[]{:S(2)}) async-start(s8[6291456]{0:T(1024)(128)(4,1)} %bitcast.144), calls=%async_computation.6 | async-start | bytes 8388608
  456.9 8.7 %slice-start.1 = ((s8[6291456]{0:T(1024)(128)(4,1)}), s8[2097152]{0:T(1024)(128)(4,1)S(1)}, s32[]{:S(2)}) async-start(s8[6291456]{0:T(1024)(128)(4,1)} %bitcast.144), calls=%async_computation.7 | async-start | bytes 4194304
  498.6 232.2 %all-gather.5.cloned.1.call-start = ((), (), s32[]{:S(2)}) async-start(), calls=%async_computation.2 | async-start | bytes 6488064 | tf_op jit(solution)/shard_map/all_gather | solution.py:79
  681.4 138.5 %reduce-scatter.2.cloned.1.call-start = ((), (), s32[]{:S(2)}) async-start(), calls=%async_computation.3 | async-start | bytes 6291456 | tf_op jit(solution)/shard_map/reduce_scatter | solution.py:95
  754.5 4.4 copy-start.3
  763.1 59.4 %copy-start.1 = (bf16[1,512,2048]{2,1,0:T(8,128)(2,1)S(1)}, bf16[1,512,2048]{2,1,0:T(8,128)(2,1)}, u32[]{:S(2)}) copy-start(bf16[1,512,2048]{2,1,0:T(8,128)(2,1)} %param.5) | copy-start | bytes 6291460
Sparse Core Ops, SparseCore 0:
  69.8 118.8 all-reduce.4
  255.8 49.2 all-gather.2
  498.8 115.6 all-reduce.6
  681.5 49.2 all-gather.4
  763.3 56.5 reduce-scatter.1
where the time goes:
time: 833 us; the launch traced here: 829 us
  waiting for transfers between devices  515 us (62%)
  blocking collectives  125 us (15%)
  matrix products  91.2 us (11%)
  local copies, waits for them, and re-layouts  51 us (6%)
  other arithmetic  28.1 us (3%)
  between operations  14.3 us (2%)
    unnamed x7, waiting for transfers between devices  226 us
    ppermute x1, waiting for transfers between devices, passed_along(): return lax.ppermute(block, axis, route)  134 us
    psum x2, blocking collectives, body(): total_sq = lax.psum(squares, 'tok')  125 us
    all_gather x2, waiting for transfers between devices, body(): weights = lax.all_gather(fresh, 'tok', axis=3, tiled=True)  98.3 us
    dot_general x15, matrix products, matmul(): jnp.dot(left, right, precision=highest, preferred_element_type=jnp.float32)  76.7 us
    reduce_scatter x1, waiting for transfers between devices, body(): lax.psum_scatter(partial_out, 'head', scatter_dimension=2, tiled=True)  56.7 us
    unnamed x23, local copies, waits for them, and re-layouts  24.5 us
    transpose x2, local copies, waits for them, and re-layouts, body(): partial_value = head_grads(weights, keys[local], targets[local])  20.6 us
  transfers between devices with their start and end apart: 6, of which 6 were waited for; matrix products, arithmetic and copies ran while one was open for 1% of the time, Pallas kernels for 0%

commit v1 on v0

--- a/solution.py
+++ b/solution.py
@@ -76,7 +76,9 @@
         own_rms = lax.dynamic_slice_in_dim(base_rms, start, width, 3)
         moved = own_weights + step_size * pieces / scale
         fresh = moved * own_rms / jnp.sqrt(jnp.mean(moved * moved, axis=2, keepdims=True) + epsilon)
-        weights = lax.all_gather(fresh, "tok", axis=3, tiled=True)
+        weights = jnp.concatenate(
+            lax.all_to_all(jnp.stack([fresh] * lax.axis_size("tok")), "tok", 0, 0), axis=3
+        )
         chosen[local] = jnp.where(position == section, weights, chosen[local])
         if section + 1 < groups:
             incoming = passed_along(weights, "block", 1)

time: 833 us -> 900 us (1.080)
  blocking collectives: 125 us -> 206 us
  waiting for transfers between devices: 515 us -> 492 us
    all_gather x2 -> x0, waiting for transfers between devices: 98.3 us -> none  [body(): weights = lax.all_gather(fresh, 'tok', axis=3, tiled=True)]
    all_to_all x0 -> x1, blocking collectives: none -> 80.5 us  [body(): lax.all_to_all(jnp.stack([fresh] * lax.axis_size('tok')), 'tok', 0, 0)]
    all_to_all x0 -> x1, waiting for transfers between devices: none -> 72.8 us  [body(): lax.all_to_all(jnp.stack([fresh] * lax.axis_size('tok')), 'tok', 0, 0)]
    unnamed x7 -> x5, waiting for transfers between devices: 226 us -> 226 us
    unnamed x23 -> x27, local copies, waits for them, and re-layouts: 24.5 us -> 24.5 us
  transfers between devices with their start and end apart: 6 -> 5, of which waited for: 6 -> 5; matrix products, arithmetic and copies ran while one was open for 1% -> 1% of each run, Pallas kernels for 0% -> 0%
where the time goes in v1:
time: 900 us; the launch traced here: 896 us
  waiting for transfers between devices  492 us (55%)
  blocking collectives  206 us (23%)
  matrix products  87 us (10%)
  local copies, waits for them, and re-layouts  55.1 us (6%)
  other arithmetic  29 us (3%)
  between operations  14.3 us (2%)
  starting transfers between devices  13.1 us (1%)
    unnamed x5, waiting for transfers between devices  226 us
    ppermute x1, waiting for transfers between devices, passed_along(): return lax.ppermute(block, axis, route)  134 us
    psum x2, blocking collectives, body(): total_sq = lax.psum(squares, 'tok')  125 us
    all_to_all x1, blocking collectives, body(): lax.all_to_all(jnp.stack([fresh] * lax.axis_size('tok')), 'tok', 0, 0)  80.5 us
    all_to_all x1, waiting for transfers between devices, body(): lax.all_to_all(jnp.stack([fresh] * lax.axis_size('tok')), 'tok', 0, 0)  72.8 us
    dot_general x15, matrix products, matmul(): jnp.dot(left, right, precision=highest, preferred_element_type=jnp.float32)  72.5 us
    reduce_scatter x1, waiting for transfers between devices, body(): lax.psum_scatter(partial_out, 'head', scatter_dimension=2, tiled=True)  59.6 us
    unnamed x27, local copies, waits for them, and re-layouts  24.5 us
  transfers between devices with their start and end apart: 5, of which 5 were waited for; matrix products, arithmetic and copies ran while one was open for 1% of the time, Pallas kernels for 0%

profile of v1, /device:TPU:1, one launch (start us, length us, event | category | flops | bytes accessed | tf_op | source)
XLA Modules:
  0.0 896.5 jit_solution(4585231092210500032)
XLA Ops:
  6.5 17.1 %copy.83 = bf16[2048,3,1024]{0,2,1:T(8,128)(2,1)} copy(bf16[2048,3,1024]{2,0,1:T(8,128)(2,1)} %param.6) | data formatting | bytes 25165824 | tf_op args[1]
  23.6 9.5 %convolution_bitcast_fusion.1 = f32[1,512,3,2,512]{1,4,3,2,0:T(8,128)S(1)} fusion(bf16[3,2,512,2048]{3,2,1,0:T(8,128)(2,1)} %bitcast.152, bf16[1,512,2048]{2,1,0:T(8,128)(2,1)S(1)} %copy-done), kind=kOutput, calls=%fused_computation.5 | convolution fusion | flops 6442450944 | bytes 20971520 | tf_op jit(solution)/shard_map/dot_general | solution.py:50
  33.7 3.6 copy-done.6
  37.3 1.8 fusion.82
  39.2 1.8 fusion.84
  41.7 1.8 fusion.80
  43.6 4.0 fusion.52
  47.5 4.5 fusion.47
  52.0 4.0 fusion.67
  56.0 3.3 maximum_bitcast_fusion
  59.3 10.3 %copy.91 = f32[2,3,512,512]{2,0,1,3:T(2,128)} copy(f32[2,3,512,512]{3,2,0,1:T(8,128)} %maximum_bitcast_fusion) | data formatting | bytes 12582912 | tf_op jit(solution)/shard_map/vmap()/transpose | solution.py:68
  69.7 3.2 copy.84
  73.0 3.5 convert_element_type.12
  77.7 0.7 multiply_reduce_fusion
  78.4 110.3 %all-reduce.5.cloned.1.call-done = f32[2,3,512,512]{2,0,1,3:T(2,128)} async-done(((f32[2,3,512,512]{2,0,1,3:T(2,128)}), f32[2,3,512,512]{2,0,1,3:T(2,128)}) %all-reduce.5.cloned.1.call-update) | async-done | bytes 6291472
  188.7 1.1 multiply_reduce_fusion.7
  189.9 62.7 %psum.14 = f32[2,3]{0,1:T(4,128)S(1)} all-reduce(f32[2,3]{0,1:T(4,128)S(1)} %get-tuple-element.9), channel_id=1, replica_groups=mesh['head'=2,'block'=2,'tok'=32] {'tok'}, use_global_device_ids=true, to_apply=%region_4.5 | all-reduce | flops 6 | bytes 48 | tf_op jit(solution)/shard_map/psum | solution.py:72
  252.7 1.1 multiply_reduce_fusion.6
  253.8 1.0 multiply_divide_fusion.1
  254.8 0.8 stack.24
  255.6 80.5 %all_to_all.10 = f32[32,2,3,512,16]{3,4,2,1,0:T(8,128)S(1)} all-to-all(f32[32,2,3,512,16]{3,4,2,1,0:T(8,128)S(1)} %stack.24), channel_id=1, replica_groups=mesh['head'=2,'block'=2,'tok'=32] {'tok'}, dimensions={0} | all-to-all | bytes 12582912 | tf_op jit(solution)/shard_map/all_to_all | solution.py:80
  336.1 1.4 copy.94
  337.5 3.9 collective-permute-start
  341.4 133.6 %collective-permute-done = f32[2,3,512,512]{2,3,1,0:T(8,128)S(1)} collective-permute-done((f32[2,3,512,512]{2,3,1,0:T(8,128)S(1)}, f32[2,3,512,512]{2,3,1,0:T(8,128)S(1)}, u32[]{:S(2)}, u32[]{:S(2)}) %collective-permute-start) | collective-permute-done | bytes 6291488 | tf_op jit(solution)/shard_map/ppermute | solution.py:14
  475.1 6.8 fusion.5
  481.9 7.0 fusion.3
  488.9 4.0 fusion.62
  492.9 6.8 fusion.4
  499.7 4.5 fusion.57
  504.2 4.0 fusion.72
  508.2 3.4 maximum_bitcast_fusion.1
  511.6 10.3 %copy.101 = f32[2,3,512,512]{2,0,1,3:T(2,128)} copy(f32[2,3,512,512]{3,2,0,1:T(8,128)} %maximum_bitcast_fusion.1) | data formatting | bytes 12582912 | tf_op jit(solution)/shard_map/vmap()/transpose | solution.py:68
  521.9 115.7 %all-reduce.7.cloned.1.call-done = f32[2,3,512,512]{2,0,1,3:T(2,128)} async-done(((f32[2,3,512,512]{2,0,1,3:T(2,128)}), f32[2,3,512,512]{2,0,1,3:T(2,128)}) %all-reduce.7.cloned.1.call-update) | async-done | bytes 6291472
  637.7 1.1 multiply_reduce_fusion.5
  638.8 62.7 %psum.15 = f32[2,3]{0,1:T(4,128)S(1)} all-reduce(f32[2,3]{0,1:T(4,128)S(1)} %get-tuple-element.7), channel_id=1, replica_groups=mesh['head'=2,'block'=2,'tok'=32] {'tok'}, use_global_device_ids=true, to_apply=%region_9.10 | all-reduce | flops 6 | bytes 48 | tf_op jit(solution)/shard_map/psum | solution.py:72
  701.6 1.1 multiply_reduce_fusion.4
  702.8 1.0 multiply_divide_fusion
  703.8 3.4 stack.29
  707.2 8.7 all-to-all-start.1
  716.4 72.8 %all-to-all-done.1 = f32[32,2,3,512,16]{3,4,2,1,0:T(8,128)} async-done(((f32[32,2,3,512,16]{3,4,2,1,0:T(8,128)}), f32[32,2,3,512,16]{3,4,2,1,0:T(8,128)}, u32[]{:S(2)}, u32[]{:S(2)}) %all-to-all-start.1) | async-done | bytes 6291488 | tf_op jit(solution)/shard_map/all_to_all | solution.py:80
  789.2 4.2 copy.104
  793.4 7.7 bitcast_select_fusion
  801.1 9.1 %fusion.2 = f32[2,512,512]{2,1,0:T(8,128)S(1)} fusion(f32[2,3,512,512]{2,3,1,0:T(8,128)} %bitcast_select_fusion, f32[1,512,3,2,512]{1,4,3,2,0:T(8,128)} %copy-done.3, f32[512,2]{0,1:T(2,128)S(1)} %add_sqrt_fusion.3), kind=kOutput, calls=%fused_computation.11 | convolution fusion | flops 3221749760 | bytes 6295552 | tf_op jit(solution)/shard_map/vmap()/dot_general | solution.py:18
  810.2 8.5 fusion.1
  818.7 4.0 multiply_reduce_fusion.1
  823.0 4.3 convolution_bitcast_fusion
  827.4 59.6 %reduce-scatter.2.cloned.1.call-done = f32[1,512,1024]{2,1,0:T(8,128)} async-done(((f32[1,512,2048]{2,1,0:T(8,128)}), f32[1,512,1024]{2,1,0:T(8,128)}) %reduce-scatter.2.cloned.1.call-update) | async-done | bytes 2097168 | tf_op jit(solution)/shard_map/reduce_scatter | solution.py:97
  887.0 2.7 convert_element_type.15
  (44 shorter events, 3.0 us)
Async XLA Ops:
  6.5 17.1 %copy-start = (bf16[1,512,2048]{2,1,0:T(8,128)(2,1)S(1)}, bf16[1,512,2048]{2,1,0:T(8,128)(2,1)}, u32[]{:S(2)}) copy-start(bf16[1,512,2048]{2,1,0:T(8,128)(2,1)} %param.5) | copy-start | bytes 6291460
  6.5 182.2 %all-reduce.5.cloned.1.call-start = ((), (), s32[]{:S(2)}) async-start(), calls=%async_computation.4 | async-start | bytes 12582912
  33.1 18.9 %copy-start.3 = (f32[1,512,3,2,512]{1,4,3,2,0:T(8,128)}, f32[1,512,3,2,512]{1,4,3,2,0:T(8,128)S(1)}, u32[]{:S(2)}) copy-start(f32[1,512,3,2,512]{1,4,3,2,0:T(8,128)S(1)} %convolution_bitcast_fusion.1) | copy-start | bytes 18874372
  33.2 4.2 copy-start.6
  39.2 1.9 copy-start.8
  69.7 568.0 %all-reduce.7.cloned.1.call-start = ((), (), s32[]{:S(2)}) async-start(), calls=%async_computation.5 | async-start | bytes 12582912
  72.9 3.5 copy-start.9
  255.6 219.5 %slice-start = ((s8[6291456]{0:T(1024)(128)(4,1)}), s8[4194304]{0:T(1024)(128)(4,1)S(1)}, s32[]{:S(2)}) async-start(s8[6291456]{0:T(1024)(128)(4,1)} %bitcast.153), calls=%async_computation.6 | async-start | bytes 8388608
  336.1 139.0 %slice-start.1 = ((s8[6291456]{0:T(1024)(128)(4,1)}), s8[2097152]{0:T(1024)(128)(4,1)S(1)}, s32[]{:S(2)}) async-start(s8[6291456]{0:T(1024)(128)(4,1)} %bitcast.153), calls=%async_computation.7 | async-start | bytes 4194304
  337.5 144.4 %copy-start.2 = (f32[32,2,3,512,16]{3,4,0,2,1:T(8,128)}, f32[32,2,3,512,16]{3,4,0,2,1:T(8,128)S(1)}, u32[]{:S(2)}) copy-start(f32[32,2,3,512,16]{3,4,0,2,1:T(8,128)S(1)} %copy.94) | copy-start | bytes 18874372
  337.5 137.6 %collective-permute-start = (f32[2,3,512,512]{2,3,1,0:T(8,128)S(1)}, f32[2,3,512,512]{2,3,1,0:T(8,128)S(1)}, u32[]{:S(2)}, u32[]{:S(2)}) collective-permute-start(f32[2,3,512,512]{2,3,1,0:T(8,128)S(1)} %bitcast.151), channel_id=1, source_target_pairs={{0,32},{1,33},{2,34},{3,35},{4,36},{5,37},{6,38},{7,39},{8,40},{9,... | collective-permute-start | bytes 18874376 | tf_op jit(solution)/shard_map/ppermute | solution.py:14
  475.1 17.8 %copy-start.7 = (f32[2,3,512,512]{2,3,1,0:T(8,128)}, f32[2,3,512,512]{2,3,1,0:T(8,128)S(1)}, u32[]{:S(2)}) copy-start(f32[2,3,512,512]{2,3,1,0:T(8,128)S(1)} %collective-permute-done) | copy-start | bytes 18874372
  707.2 82.0 %all-to-all-start.1 = ((f32[32,2,3,512,16]{3,4,2,1,0:T(8,128)}), f32[32,2,3,512,16]{3,4,2,1,0:T(8,128)}, u32[]{:S(2)}, u32[]{:S(2)}) async-start(f32[32,2,3,512,16]{3,4,2,1,0:T(8,128)} %stack.29), calls=%async_computation.1 | async-start | bytes 12582912 | tf_op jit(solution)/shard_map/all_to_all | solution.py:80
  715.9 171.2 %reduce-scatter.2.cloned.1.call-start = ((), (), s32[]{:S(2)}) async-start(), calls=%async_computation.3 | async-start | bytes 6291456 | tf_op jit(solution)/shard_map/reduce_scatter | solution.py:97
  801.1 9.1 %copy-start.5 = (f32[2,3,512,512]{2,3,1,0:T(8,128)S(1)}, f32[2,3,512,512]{2,3,1,0:T(8,128)}, u32[]{:S(2)}) copy-start(f32[2,3,512,512]{2,3,1,0:T(8,128)} %bitcast_select_fusion) | copy-start | bytes 18874372
  818.7 4.3 copy-start.4
  827.4 62.4 %copy-start.1 = (bf16[1,512,2048]{2,1,0:T(8,128)(2,1)S(1)}, bf16[1,512,2048]{2,1,0:T(8,128)(2,1)}, u32[]{:S(2)}) copy-start(bf16[1,512,2048]{2,1,0:T(8,128)(2,1)} %param.5) | copy-start | bytes 6291460
Sparse Core Ops, SparseCore 0:
  69.8 118.8 all-reduce.4
  522.1 115.5 all-reduce.6
  827.5 59.4 reduce-scatter.1
